TPU v7x, 32 devices: a whole 2x2x4 slice. The times are simulated.
32 devices in a mesh: ctx: 16 (over z, y, x), fsdp: 2 (over core).
Axes of the slice: x: 2, y: 2, z: 4, core: 2. Of those that a mesh axis runs over, the one named last changes fastest.
Arguments:
- block_input: bfloat16 [4, 1024, 1024], P('fsdp', 'ctx'), may hold values from -6 to 6
- cotangent: bfloat16 [4, 1024, 1024], P('fsdp', 'ctx'), may hold values from -6 to 6
- block_table: int32 [16, 2], replicated, may hold values from 0 to 31, as said below
- segments: int32 [4, 1024], P('fsdp'), may hold values from 0 to 2, as said below
- gain_one: bfloat16 [1024], P('fsdp'), may hold values from 0.25 to 1.75
- shift_one: bfloat16 [1024], P('fsdp'), may hold values from -3 to 3
- w_mix: bfloat16 [1024, 3072], P('fsdp'), may hold values from -0.1875 to 0.1875
- bias_query: bfloat16 [1024], P('fsdp'), may hold values from -3 to 3
- bias_value: bfloat16 [1024], P('fsdp'), may hold values from -3 to 3
- w_merge: bfloat16 [1024, 1024], P('fsdp'), may hold values from -0.375 to 0.375
- bias_merge: bfloat16 [1024], P('fsdp'), may hold values from -3 to 3
- gain_two: bfloat16 [1024], P('fsdp'), may hold values from 0.25 to 1.75
- shift_two: bfloat16 [1024], P('fsdp'), may hold values from -3 to 3
- w_expand: bfloat16 [1024, 4096], P('fsdp'), may hold values from -0.1875 to 0.1875
- bias_expand: bfloat16 [4096], P('fsdp'), may hold values from -3 to 3
- w_reduce: bfloat16 [4096, 1024], P('fsdp'), may hold values from -0.09375 to 0.09375
- bias_reduce: bfloat16 [1024], P('fsdp'), may hold values from -3 to 3
Outputs:
- block_output: bfloat16 [4, 1024, 1024], P('fsdp', 'ctx')
- grad_input: float32 [4, 1024, 1024], P('fsdp', 'ctx')
- grad_gain_one: float32 [1024], P(('ctx', 'fsdp'))
- grad_shift_one: float32 [1024], P(('ctx', 'fsdp'))
- grad_w_mix: float32 [1024, 3072], P(('ctx', 'fsdp'))
- grad_bias_query: float32 [1024], P(('ctx', 'fsdp'))
- grad_bias_value: float32 [1024], P(('ctx', 'fsdp'))
- grad_w_merge: float32 [1024, 1024], P(('ctx', 'fsdp'))
- grad_bias_merge: float32 [1024], P(('ctx', 'fsdp'))
- grad_gain_two: float32 [1024], P(('ctx', 'fsdp'))
- grad_shift_two: float32 [1024], P(('ctx', 'fsdp'))
- grad_w_expand: float32 [1024, 4096], P(('ctx', 'fsdp'))
- grad_bias_expand: float32 [4096], P(('ctx', 'fsdp'))
- grad_w_reduce: float32 [4096, 1024], P(('ctx', 'fsdp'))
- grad_bias_reduce: float32 [1024], P(('ctx', 'fsdp'))
Inputs may be any that keep to these rules, and one draw needn't show every extreme that they name: `block_table`: row c lists the two blocks of 32 positions that the slots of index c of ctx hold, in slot order: a block b below 16, then its mirror 2 * 16 - 1 - b; every block appears once. `segments`: document ids by slot. Taken in order of position (slot s holds position block_table[s // 64, (s // 32) % 2] * 32 + s % 32), the ids of a sequence never fall, and each of its 3 documents holds at least one position.
All inputs are finite; a program needn't handle non-finite values.
Results may differ from a plain program's by a relative error of at most 0.02.
Values may be sent and summed in bfloat16 or wider, within the bound.
A program may use at most 320 MiB of HBM per device.

v0:
```python
import math
import jax
import jax.numpy as jnp
from jax import lax
from jax.sharding import PartitionSpec as P

HEADS = 16
EPSILON = 1e-05
CUBIC = 0.044715
ROOT = math.sqrt(2.0 / math.pi)


def gelu_value(pre):
    inner = ROOT * (pre + CUBIC * pre * pre * pre)
    return 0.5 * pre * (1.0 + jnp.tanh(inner))


def gelu_slope(pre):
    inner = ROOT * (pre + CUBIC * pre * pre * pre)
    tangent = jnp.tanh(inner)
    return 0.5 * (1.0 + tangent) + 0.5 * pre * (1.0 - tangent * tangent) * ROOT * (
        1.0 + 3.0 * CUBIC * pre * pre
    )


def norm_forward(rows, gain, shift):
    center = rows - jnp.mean(rows, axis=-1, keepdims=True)
    inverse = lax.rsqrt(jnp.mean(center * center, axis=-1, keepdims=True) + EPSILON)
    normed = center * inverse
    return (
        normed,
        inverse,
        (normed * gain.astype(jnp.float32) + shift.astype(jnp.float32)).astype(jnp.bfloat16),
    )


def norm_backward(grad, normed, inverse, gain):
    scaled = grad * gain.astype(jnp.float32)
    return inverse * (
        scaled
        - jnp.mean(scaled, axis=-1, keepdims=True)
        - normed * jnp.mean(scaled * normed, axis=-1, keepdims=True)
    )


def slot_positions(block_table, block):
    blocks = block_table.reshape(-1)
    return (blocks[:, None] * block + jnp.arange(block, dtype=jnp.int32)[None, :]).reshape(-1)


def body(
    block_input,
    cotangent,
    block_table,
    segments,
    gain_one,
    shift_one,
    w_mix,
    bias_query,
    bias_value,
    w_merge,
    bias_merge,
    gain_two,
    shift_two,
    w_expand,
    bias_expand,
    w_reduce,
    bias_reduce,
):
    groups, width, model = block_input.shape
    length = segments.shape[1]
    heads = HEADS
    head = model // heads
    half_heads = heads // 2
    scale = 1.0 / math.sqrt(head)
    (
        gain_one,
        shift_one,
        w_mix,
        bias_query,
        bias_value,
        w_merge,
        bias_merge,
        gain_two,
        shift_two,
        w_expand,
        bias_expand,
        w_reduce,
        bias_reduce,
    ) = (
        lax.all_gather(gain_one, "fsdp", axis=0, tiled=True),
        lax.all_gather(shift_one, "fsdp", axis=0, tiled=True),
        lax.all_gather(w_mix, "fsdp", axis=0, tiled=True),
        lax.all_gather(bias_query, "fsdp", axis=0, tiled=True),
        lax.all_gather(bias_value, "fsdp", axis=0, tiled=True),
        lax.all_gather(w_merge, "fsdp", axis=0, tiled=True),
        lax.all_gather(bias_merge, "fsdp", axis=0, tiled=True),
        lax.all_gather(gain_two, "fsdp", axis=0, tiled=True),
        lax.all_gather(shift_two, "fsdp", axis=0, tiled=True),
        lax.all_gather(w_expand, "fsdp", axis=0, tiled=True),
        lax.all_gather(bias_expand, "fsdp", axis=0, tiled=True),
        lax.all_gather(w_reduce, "fsdp", axis=0, tiled=True),
        lax.all_gather(bias_reduce, "fsdp", axis=0, tiled=True),
    )
    key_position = slot_positions(block_table, width // 2)
    first_slot = lax.axis_index("ctx") * width
    query_position = lax.dynamic_slice_in_dim(key_position, first_slot, width)
    query_segment = lax.dynamic_slice_in_dim(segments, first_slot, width, axis=1)
    visible = jnp.logical_and(
        key_position[None, None, :] <= query_position[None, :, None],
        segments[:, None, :] == query_segment[:, :, None],
    )
    tokens = block_input.reshape(groups * width, model).astype(jnp.float32)
    normed_one, inverse_one, first_in = norm_forward(tokens, gain_one, shift_one)
    offsets = jnp.concatenate([bias_query, jnp.zeros_like(bias_query), bias_value]).astype(
        jnp.float32
    )
    mixed = (jnp.dot(first_in, w_mix, preferred_element_type=jnp.float32) + offsets).astype(
        jnp.bfloat16
    )
    queries = mixed[:, :model].reshape(groups, width, heads, head)
    local_pairs = mixed[:, model:].reshape(groups, width, 2 * model)
    pairs = lax.all_gather(local_pairs, "ctx", axis=1, tiled=True)
    keys = pairs[:, :, :model].reshape(groups, length, heads, head)
    values = pairs[:, :, model:].reshape(groups, length, heads, head)
    context_parts, log_parts = ([], [])
    for half in range(2):
        first = half * half_heads
        part_scores = (
            jnp.einsum(
                "gshd,gthd->ghst",
                queries[:, :, first : first + half_heads],
                keys[:, :, first : first + half_heads],
                preferred_element_type=jnp.float32,
            )
            * scale
        )
        expo = jnp.where(visible[:, None], jnp.exp(part_scores), 0.0)
        total = jnp.sum(expo, axis=-1)
        summed = jnp.einsum(
            "ghst,gthd->gshd",
            expo.astype(jnp.bfloat16),
            values[:, :, first : first + half_heads],
            preferred_element_type=jnp.float32,
        )
        context_parts.append(summed / jnp.swapaxes(total, 1, 2)[..., None])
        log_parts.append(jnp.log(total))
    context = jnp.concatenate(context_parts, axis=2).astype(jnp.bfloat16)
    log_total = jnp.concatenate(log_parts, axis=1)
    context_rows = context.reshape(groups * width, model)
    resid = (
        tokens
        + jnp.dot(context_rows, w_merge, preferred_element_type=jnp.float32)
        + bias_merge.astype(jnp.float32)
    )
    normed_two, inverse_two, second_in = norm_forward(resid, gain_two, shift_two)
    pre = jnp.dot(second_in, w_expand, preferred_element_type=jnp.float32) + bias_expand.astype(
        jnp.float32
    )
    act = gelu_value(pre).astype(jnp.bfloat16)
    block_output = (
        resid
        + jnp.dot(act, w_reduce, preferred_element_type=jnp.float32)
        + bias_reduce.astype(jnp.float32)
    ).astype(jnp.bfloat16)
    upstream = cotangent.reshape(groups * width, model)
    incoming = upstream.astype(jnp.float32)
    grad_reduce = jnp.einsum("ti,tj->ij", act, upstream, preferred_element_type=jnp.float32)
    grad_pre = jnp.einsum(
        "tj,ij->ti", upstream, w_reduce, preferred_element_type=jnp.float32
    ) * gelu_slope(pre)
    pre_rounded = grad_pre.astype(jnp.bfloat16)
    grad_expand = jnp.einsum(
        "ti,tj->ij", second_in, pre_rounded, preferred_element_type=jnp.float32
    )
    grad_second = jnp.einsum("tj,ij->ti", pre_rounded, w_expand, preferred_element_type=jnp.float32)
    grad_resid = incoming + norm_backward(grad_second, normed_two, inverse_two, gain_two)
    feed = (
        lax.psum_scatter(
            jnp.sum(grad_second * normed_two, axis=0),
            ("ctx", "fsdp"),
            scatter_dimension=0,
            tiled=True,
        ),
        lax.psum_scatter(
            jnp.sum(grad_second, axis=0), ("ctx", "fsdp"), scatter_dimension=0, tiled=True
        ),
        lax.psum_scatter(grad_expand, ("ctx", "fsdp"), scatter_dimension=0, tiled=True),
        lax.psum_scatter(
            jnp.sum(grad_pre, axis=0), ("ctx", "fsdp"), scatter_dimension=0, tiled=True
        ),
        lax.psum_scatter(grad_reduce, ("ctx", "fsdp"), scatter_dimension=0, tiled=True),
        lax.psum_scatter(
            jnp.sum(incoming, axis=0), ("ctx", "fsdp"), scatter_dimension=0, tiled=True
        ),
    )
    resid_rounded = grad_resid.astype(jnp.bfloat16)
    grad_merge = jnp.einsum(
        "ti,tj->ij", context_rows, resid_rounded, preferred_element_type=jnp.float32
    )
    grad_context = jnp.einsum(
        "tj,ij->ti", resid_rounded, w_merge, preferred_element_type=jnp.float32
    ).astype(jnp.bfloat16)
    delta = jnp.sum(
        (grad_context.astype(jnp.float32) * context_rows.astype(jnp.float32)).reshape(
            groups, width, heads, head
        ),
        axis=-1,
    )
    delta = jnp.swapaxes(delta, 1, 2)
    grad_heads = grad_context.reshape(groups, width, heads, head)
    query_parts, key_parts, value_parts = ([], [], [])
    for half in range(2):
        first = half * half_heads
        query_part = queries[:, :, first : first + half_heads]
        key_part = keys[:, :, first : first + half_heads]
        value_part = values[:, :, first : first + half_heads]
        grad_part = grad_heads[:, :, first : first + half_heads]
        part_scores = (
            jnp.einsum("gshd,gthd->ghst", query_part, key_part, preferred_element_type=jnp.float32)
            * scale
        )
        prob = jnp.where(
            visible[:, None],
            jnp.exp(part_scores - log_total[:, first : first + half_heads, :, None]),
            0.0,
        )
        dprob = jnp.einsum(
            "gshd,gthd->ghst", grad_part, value_part, preferred_element_type=jnp.float32
        )
        grad_score = prob * (dprob - delta[:, first : first + half_heads, :, None])
        score_rounded = grad_score.astype(jnp.bfloat16)
        query_parts.append(
            jnp.einsum(
                "ghst,gthd->gshd", score_rounded, key_part, preferred_element_type=jnp.float32
            )
            * scale
        )
        key_term = (
            jnp.einsum(
                "ghst,gshd->gthd", score_rounded, query_part, preferred_element_type=jnp.float32
            )
            * scale
        )
        value_term = jnp.einsum(
            "ghst,gshd->gthd",
            prob.astype(jnp.bfloat16),
            grad_part,
            preferred_element_type=jnp.float32,
        )
        key_sum, value_sum = (
            lax.psum_scatter(
                key_term.reshape(groups, length, half_heads * head),
                "ctx",
                scatter_dimension=1,
                tiled=True,
            ),
            lax.psum_scatter(
                value_term.reshape(groups, length, half_heads * head),
                "ctx",
                scatter_dimension=1,
                tiled=True,
            ),
        )
        key_parts.append(key_sum)
        value_parts.append(value_sum)
    grad_query = jnp.concatenate(query_parts, axis=2)
    grad_key = jnp.concatenate(key_parts, axis=2)
    grad_value = jnp.concatenate(value_parts, axis=2)
    query_rows_grad = grad_query.reshape(groups * width, model)
    key_rows_grad = grad_key.reshape(groups * width, model)
    value_rows_grad = grad_value.reshape(groups * width, model)
    grad_mixed = jnp.concatenate([query_rows_grad, key_rows_grad, value_rows_grad], axis=1).astype(
        jnp.bfloat16
    )
    grad_mix = jnp.einsum("ti,tj->ij", first_in, grad_mixed, preferred_element_type=jnp.float32)
    grad_first = jnp.einsum("tj,ij->ti", grad_mixed, w_mix, preferred_element_type=jnp.float32)
    grad_tokens = grad_resid + norm_backward(grad_first, normed_one, inverse_one, gain_one)
    front = (
        lax.psum_scatter(
            jnp.sum(grad_first * normed_one, axis=0),
            ("ctx", "fsdp"),
            scatter_dimension=0,
            tiled=True,
        ),
        lax.psum_scatter(
            jnp.sum(grad_first, axis=0), ("ctx", "fsdp"), scatter_dimension=0, tiled=True
        ),
        lax.psum_scatter(grad_mix, ("ctx", "fsdp"), scatter_dimension=0, tiled=True),
        lax.psum_scatter(
            jnp.sum(query_rows_grad, axis=0), ("ctx", "fsdp"), scatter_dimension=0, tiled=True
        ),
        lax.psum_scatter(
            jnp.sum(value_rows_grad, axis=0), ("ctx", "fsdp"), scatter_dimension=0, tiled=True
        ),
        lax.psum_scatter(grad_merge, ("ctx", "fsdp"), scatter_dimension=0, tiled=True),
        lax.psum_scatter(
            jnp.sum(grad_resid, axis=0), ("ctx", "fsdp"), scatter_dimension=0, tiled=True
        ),
    )
    return (
        block_output.reshape(groups, width, model),
        grad_tokens.reshape(groups, width, model),
        front[0],
        front[1],
        front[2],
        front[3],
        front[4],
        front[5],
        front[6],
        feed[0],
        feed[1],
        feed[2],
        feed[3],
        feed[4],
        feed[5],
    )


def solution(mesh):
    in_specs = (
        P("fsdp", "ctx", None),
        P("fsdp", "ctx", None),
        P(),
        P("fsdp", None),
        P("fsdp"),
        P("fsdp"),
        P("fsdp", None),
        P("fsdp"),
        P("fsdp"),
        P("fsdp", None),
        P("fsdp"),
        P("fsdp"),
        P("fsdp"),
        P("fsdp", None),
        P("fsdp"),
        P("fsdp", None),
        P("fsdp"),
    )
    out_specs = (
        P("fsdp", "ctx", None),
        P("fsdp", "ctx", None),
        P(("ctx", "fsdp")),
        P(("ctx", "fsdp")),
        P(("ctx", "fsdp"), None),
        P(("ctx", "fsdp")),
        P(("ctx", "fsdp")),
        P(("ctx", "fsdp"), None),
        P(("ctx", "fsdp")),
        P(("ctx", "fsdp")),
        P(("ctx", "fsdp")),
        P(("ctx", "fsdp"), None),
        P(("ctx", "fsdp")),
        P(("ctx", "fsdp"), None),
        P(("ctx", "fsdp")),
    )
    return jax.shard_map(body, mesh=mesh, in_specs=in_specs, out_specs=out_specs, check_vma=False)
```

profile of v0, /device:TPU:13, one launch (start us, length us, event | category | flops | bytes accessed | tf_op | source)
XLA Modules:
  0.0 1311.0 jit_solution(4099106619607151137)
XLA Ops:
  8.6 2.2 all-gather.1
  22.2 6.0 all-gather.14.cloned.1.call-done
  28.2 3.8 fusion
  34.8 1.8 all-gather.4
  43.5 99.3 %all-gather.16.cloned.1.call-done = bf16[2,1024,2048]{2,1,0:T(8,128)(2,1)} async-done(((bf16[2,64,2048]{2,1,0:T(8,128)(2,1)}), bf16[2,1024,2048]{2,1,0:T(8,128)(2,1)}) %all-gather.16.cloned.1.call-update) | async-done | bytes 8388624 | tf_op jit(solution)/shard_map/all_gather | solution.py:123
  142.8 5.9 fusion.95
  148.7 6.4 copy.60
  155.1 6.2 copy.63
  161.4 2.4 fusion.22
  164.2 2.4 fusion.1
  171.5 2.4 fusion.100
  174.2 5.0 all-gather.20.cloned.1.call-done
  179.1 4.8 convolution_add_fusion
  183.9 17.7 %all-gather.22.cloned.1.call-done = bf16[4096,1024]{1,0:T(8,128)(2,1)} async-done(((bf16[2048,1024]{1,0:T(8,128)(2,1)}), bf16[4096,1024]{1,0:T(8,128)(2,1)}) %all-gather.22.cloned.1.call-update) | async-done | bytes 8388624 | tf_op jit(solution)/shard_map/all_gather | solution.py:102
  201.6 7.6 fusion.101
  209.3 3.5 multiply_reduce_fusion
  216.0 2.1 reshape.251
  218.1 1.9 fusion.97
  220.0 2.4 reshape.252
  222.4 2.2 reduce_sum.190
  227.7 5.1 multiply_convert_fusion
  232.8 2.7 convolution_multiply_fusion.1
  235.5 5.4 copy.74
  243.8 4.6 multiply_convert_fusion.1
  249.7 2.7 convolution_multiply_fusion.2
  252.4 5.4 copy.72
  257.9 5.2 fusion.14
  263.1 5.4 copy.76
  268.6 5.2 fusion.12
  273.8 5.4 copy.78
  279.3 3.8 fusion.80
  283.3 3.1 fusion.49
  290.2 2.1 reshape.253
  292.4 42.6 %reduce-scatter.11.cloned.1.call-done = f32[2,64,512]{2,1,0:T(8,128)} async-done(((f32[2,1024,512]{2,1,0:T(8,128)}), f32[2,64,512]{2,1,0:T(8,128)}) %reduce-scatter.11.cloned.1.call-update) | async-done | bytes 262160 | tf_op jit(solution)/shard_map/reduce_scatter | solution.py:252
  336.0 96.1 %reduce-scatter.9.cloned.1.call-done = f32[2,64,512]{2,1,0:T(8,128)} async-done(((f32[2,1024,512]{2,1,0:T(8,128)}), f32[2,64,512]{2,1,0:T(8,128)}) %reduce-scatter.9.cloned.1.call-update) | async-done | bytes 262160 | tf_op jit(solution)/shard_map/reduce_scatter | solution.py:252
  433.8 95.4 %reduce-scatter.13.cloned.1.call-done = f32[2,64,512]{2,1,0:T(8,128)} async-done(((f32[2,1024,512]{2,1,0:T(8,128)}), f32[2,64,512]{2,1,0:T(8,128)}) %reduce-scatter.13.cloned.1.call-update) | async-done | bytes 262160 | tf_op jit(solution)/shard_map/reduce_scatter | solution.py:258
  530.8 95.4 %reduce-scatter.15.cloned.1.call-done = f32[2,64,512]{2,1,0:T(8,128)} async-done(((f32[2,1024,512]{2,1,0:T(8,128)}), f32[2,64,512]{2,1,0:T(8,128)}) %reduce-scatter.15.cloned.1.call-update) | async-done | bytes 262160 | tf_op jit(solution)/shard_map/reduce_scatter | solution.py:258
  629.9 7.4 fusion.70
  638.0 9.4 fusion.66
  647.4 9.1 fusion.93
  657.2 2.1 all-gather.7
  661.7 5.7 fusion.48
  667.5 5.2 multiply_reduce_fusion.1
  672.7 41.6 %all-reduce.9 = (f32[1024]{0:T(1024)S(1)}, f32[1024]{0:T(1024)S(1)}, f32[1024]{0:T(1024)S(1)}, f32[1024]{0:T(1024)S(1)}, f32[1024]{0:T(1024)S(1)}, /*index=5*/f3...) all-reduce(f32[1024]{0:T(1024)S(1)} %get-tuple-element.17, ...), channel_id=6, replica_groups=mesh['ctx'=16,'fsdp'=2] {'ctx','fsdp'}, use_global_device_ids=true, to_apply=%region_16.17.clone | all-reduce | flops 12288 | bytes 98304
  720.6 19.2 %reduce-scatter.19.cloned.1.call-done = f32[32,1024]{1,0:T(8,128)} async-done(((f32[1024,1024]{1,0:T(8,128)}), f32[32,1024]{1,0:T(8,128)}) %reduce-scatter.19.cloned.1.call-update) | async-done | bytes 131088 | tf_op jit(solution)/shard_map/reduce_scatter | solution.py:296
  739.8 188.1 %reduce-scatter.17.cloned.1.call-done = f32[32,3072]{1,0:T(8,128)} async-done(((f32[1024,3072]{1,0:T(8,128)}), f32[32,3072]{1,0:T(8,128)}) %reduce-scatter.17.cloned.1.call-update) | async-done | bytes 393232 | tf_op jit(solution)/shard_map/reduce_scatter | solution.py:289
  927.9 188.8 %reduce-scatter.21.cloned.1.call-done = f32[32,4096]{1,0:T(8,128)} async-done(((f32[1024,4096]{1,0:T(8,128)}), f32[32,4096]{1,0:T(8,128)}) %reduce-scatter.21.cloned.1.call-update) | async-done | bytes 524304 | tf_op jit(solution)/shard_map/reduce_scatter | solution.py:188
  1116.8 187.5 %reduce-scatter.23.cloned.1.call-done = f32[128,1024]{1,0:T(8,128)} async-done(((f32[4096,1024]{1,0:T(8,128)}), f32[128,1024]{1,0:T(8,128)}) %reduce-scatter.23.cloned.1.call-update) | async-done | bytes 524304 | tf_op jit(solution)/shard_map/reduce_scatter | solution.py:192
  (204 shorter events, 60.5 us)
Async XLA Ops:
  7.2 21.0 %all-gather.14.cloned.1.call-start = ((), (), s32[]{:S(2)}) async-start(), calls=%async_computation.8 | async-start | bytes 9437184 | tf_op jit(solution)/shard_map/all_gather | solution.py:93
  7.9 134.9 %all-gather.16.cloned.1.call-start = ((), (), s32[]{:S(2)}) async-start(), calls=%async_computation.9 | async-start | bytes 8912896 | tf_op jit(solution)/shard_map/all_gather | solution.py:123
  14.5 7.6 copy-start.36
  15.7 6.4 copy-start.38
  22.1 9.8 copy-start.11
  32.8 138.7 %all-gather.18.cloned.1.call-start = ((), (), s32[]{:S(2)}) async-start(), calls=%async_computation.10 | async-start | bytes 3145728 | tf_op jit(solution)/shard_map/all_gather | solution.py:96
  33.5 3.1 copy-start.44
  33.6 3.5 copy-start.35
  33.6 5.3 copy-start.41
  33.6 7.1 copy-start.42
  33.6 9.1 copy-start.33
  33.6 145.5 %all-gather.20.cloned.1.call-start = ((), (), s32[]{:S(2)}) async-start(), calls=%async_computation.11 | async-start | bytes 12582912 | tf_op jit(solution)/shard_map/all_gather | solution.py:100
  34.2 167.4 %all-gather.22.cloned.1.call-start = ((), (), s32[]{:S(2)}) async-start(), calls=%async_computation.12 | async-start | bytes 12582912 | tf_op jit(solution)/shard_map/all_gather | solution.py:102
  34.8 300.2 %reduce-scatter.11.cloned.1.call-start = ((), (), s32[]{:S(2)}) async-start(), calls=%async_computation.14 | async-start | bytes 4456448 | tf_op jit(solution)/shard_map/reduce_scatter | solution.py:252
  43.5 117.9 %copy-start.14 = (bf16[2,64,8,64]{3,2,1,0:T(8,128)(2,1)}, bf16[2,64,8,64]{3,2,1,0:T(8,128)(2,1)S(1)}, u32[]{:S(2)}) copy-start(bf16[2,64,8,64]{3,2,1,0:T(8,128)(2,1)S(1)} %get-tuple-element.43) | copy-start | bytes 393220
  43.5 120.3 %copy-start.21 = (bf16[2,64,8,64]{3,2,1,0:T(8,128)(2,1)}, bf16[2,64,8,64]{3,2,1,0:T(8,128)(2,1)S(1)}, u32[]{:S(2)}) copy-start(bf16[2,64,8,64]{3,2,1,0:T(8,128)(2,1)S(1)} %get-tuple-element.42) | copy-start | bytes 393220
  163.8 3.5 copy-start.1
  164.2 4.6 copy-start.10
  166.6 3.0 copy-start.9
  166.6 3.0 copy-start.34
  171.5 7.7 copy-start.7
  174.1 35.1 %copy-start.27 = (f32[128]{0:T(128)}, f32[128]{0:T(128)S(1)}, u32[]{:S(2)}) copy-start(f32[128]{0:T(128)S(1)} %add_rsqrt_fusion.1) | copy-start | bytes 1540
  179.1 22.4 %copy-start.12 = (bf16[2,64,1024]{2,1,0:T(8,128)(2,1)S(1)}, bf16[2,64,1024]{2,1,0:T(8,128)(2,1)}, u32[]{:S(2)}) copy-start(bf16[2,64,1024]{2,1,0:T(8,128)(2,1)} %param.18) | copy-start | bytes 786436
  201.6 7.7 copy-start
  209.2 3.6 copy-start.6
  209.2 3.6 copy-start.13
  209.2 5.1 copy-start.4
  209.2 5.0 copy-start.8
  227.7 5.1 copy-start.15
  240.9 191.1 %reduce-scatter.9.cloned.1.call-start = ((), (), s32[]{:S(2)}) async-start(), calls=%async_computation.13 | async-start | bytes 4456448 | tf_op jit(solution)/shard_map/reduce_scatter | solution.py:252
  243.8 5.9 copy-start.22
  257.9 271.3 %reduce-scatter.13.cloned.1.call-start = ((), (), s32[]{:S(2)}) async-start(), calls=%async_computation.15 | async-start | bytes 4456448 | tf_op jit(solution)/shard_map/reduce_scatter | solution.py:258
  268.6 357.7 %reduce-scatter.15.cloned.1.call-start = ((), (), s32[]{:S(2)}) async-start(), calls=%async_computation.16 | async-start | bytes 4456448 | tf_op jit(solution)/shard_map/reduce_scatter | solution.py:258
  279.3 460.6 %reduce-scatter.19.cloned.1.call-start = ((), (), s32[]{:S(2)}) async-start(), calls=%async_computation.18 | async-start | bytes 4325376 | tf_op jit(solution)/shard_map/reduce_scatter | solution.py:296
  283.1 644.8 %reduce-scatter.17.cloned.1.call-start = ((), (), s32[]{:S(2)}) async-start(), calls=%async_computation.17 | async-start | bytes 12976128 | tf_op jit(solution)/shard_map/reduce_scatter | solution.py:289
  283.3 3.5 copy-start.3
  283.3 4.2 copy-start.18
  637.3 479.4 %reduce-scatter.21.cloned.1.call-start = ((), (), s32[]{:S(2)}) async-start(), calls=%async_computation.19 | async-start | bytes 17301504 | tf_op jit(solution)/shard_map/reduce_scatter | solution.py:188
  647.4 656.9 %reduce-scatter.23.cloned.1.call-start = ((), (), s32[]{:S(2)}) async-start(), calls=%async_computation.20 | async-start | bytes 17301504 | tf_op jit(solution)/shard_map/reduce_scatter | solution.py:192
  661.7 5.7 copy-start.23
  661.7 5.7 copy-start.25
  661.7 5.7 copy-start.26
  661.7 5.7 copy-start.37
  661.7 5.7 copy-start.39
  667.4 5.2 copy-start.29
  667.5 5.2 copy-start.30
  667.5 5.2 copy-start.31
  667.5 5.2 copy-start.32
  (10 other events, 13.7 us)
Sparse Core Ops, SparseCore 0:
  9.5 18.5 all-gather.13
  32.9 109.8 all-gather.15
  144.3 12.2 all-gather.17
  158.1 21.0 all-gather.19
  180.5 21.0 all-gather.21
  241.1 93.9 reduce-scatter.10
  337.3 94.7 reduce-scatter.8
  434.4 94.7 reduce-scatter.12
  531.5 94.7 reduce-scatter.14
  629.0 110.8 reduce-scatter.18
  746.4 181.4 reduce-scatter.16
  930.7 186.0 reduce-scatter.20
  1119.6 184.5 reduce-scatter.22
where the time goes:
time: 1320 us; the launch traced here: 1310 us
  waiting for transfers between devices  1040 us (79%)
  matrix products  100 us (8%)
  local copies, waits for them, and re-layouts  77.6 us (6%)
  blocking collectives  58.6 us (4%)
  other arithmetic  15.4 us (1%)
  between operations  14.8 us (1%)
    reduce_scatter x2, waiting for transfers between devices, body(): lax.psum_scatter(value_term.reshape(groups, length, half_heads * head), '...  191 us
    reduce_scatter x1, waiting for transfers between devices, body(): lax.psum_scatter(grad_expand, ('ctx', 'fsdp'), scatter_dimension=0, tiled...  189 us
    reduce_scatter x1, waiting for transfers between devices, body(): lax.psum_scatter(grad_mix, ('ctx', 'fsdp'), scatter_dimension=0, tiled=True)  188 us
    reduce_scatter x1, waiting for transfers between devices, body(): lax.psum_scatter(grad_reduce, ('ctx', 'fsdp'), scatter_dimension=0, tiled...  188 us
    reduce_scatter x2, waiting for transfers between devices, body(): lax.psum_scatter(key_term.reshape(groups, length, half_heads * head), 'ct...  139 us
    all_gather x1, waiting for transfers between devices, body(): pairs = lax.all_gather(local_pairs, 'ctx', axis=1, tiled=True)  99.3 us
    unnamed x1, blocking collectives  41.6 us
  transfers between devices with their start and end apart: 13, of which 12 were waited for; matrix products, arithmetic and copies ran while one was open for 11% of the time, Pallas kernels for 0%

commit v1 on v0

--- a/solution.py
+++ b/solution.py
@@ -120,7 +120,16 @@
     )
     queries = mixed[:, :model].reshape(groups, width, heads, head)
     local_pairs = mixed[:, model:].reshape(groups, width, 2 * model)
-    pairs = lax.all_gather(local_pairs, "ctx", axis=1, tiled=True)
+    ways = lax.axis_size("ctx")
+    up = [(d, (d + 1) % ways) for d in range(ways)]
+    down = [(d, (d - 1) % ways) for d in range(ways)]
+    earlier, later = ([local_pairs], [local_pairs])
+    for _ in range(ways // 2):
+        earlier.append(lax.ppermute(earlier[-1], "ctx", up))
+    for _ in range((ways - 1) // 2):
+        later.append(lax.ppermute(later[-1], "ctx", down))
+    line = jnp.concatenate([*earlier[::-1], *later[1:]], axis=1)
+    pairs = jnp.roll(line, (lax.axis_index("ctx") - ways // 2) * local_pairs.shape[1], axis=1)
     keys = pairs[:, :, :model].reshape(groups, length, heads, head)
     values = pairs[:, :, model:].reshape(groups, length, heads, head)
     context_parts, log_parts = ([], [])

time: 1320 us -> 1420 us (1.076)
  local copies, waits for them, and re-layouts: 77.6 us -> 119 us
  waiting for transfers between devices: 1040 us -> 1080 us
    ppermute x0 -> x15, waiting for transfers between devices: none -> 141 us  [the longest x7 105 us: body(): later.append(lax.ppermute(later[-1], 'ctx', down))]
    all_gather x1 -> x0, waiting for transfers between devices: 99.3 us -> none  [body(): pairs = lax.all_gather(local_pairs, 'ctx', axis=1, tiled=True)]
    unnamed x110 -> x163, local copies, waits for them, and re-layouts: 16.9 us -> 56.6 us
    all_gather x1, waiting for transfers between devices: 17.7 us -> 0.02 us  [body(): lax.all_gather(w_reduce, 'fsdp', axis=0, tiled=True)]
  transfers between devices with their start and end apart: 13 -> 27, of which waited for: 12 -> 19; matrix products, arithmetic and copies ran while one was open for 11% -> 13% of each run, Pallas kernels for 0% -> 0%
where the time goes in v1:
time: 1420 us; the launch traced here: 1410 us
  waiting for transfers between devices  1080 us (76%)
  local copies, waits for them, and re-layouts  119 us (8%)
  matrix products  100 us (7%)
  blocking collectives  69.7 us (5%)
  between operations  15.3 us (1%)
  starting transfers between devices  14.7 us (1%)
    reduce_scatter x2, waiting for transfers between devices, body(): lax.psum_scatter(value_term.reshape(groups, length, half_heads * head), '...  191 us
    reduce_scatter x1, waiting for transfers between devices, body(): lax.psum_scatter(grad_expand, ('ctx', 'fsdp'), scatter_dimension=0, tiled...  189 us
    reduce_scatter x1, waiting for transfers between devices, body(): lax.psum_scatter(grad_mix, ('ctx', 'fsdp'), scatter_dimension=0, tiled=True)  188 us
    reduce_scatter x1, waiting for transfers between devices, body(): lax.psum_scatter(grad_reduce, ('ctx', 'fsdp'), scatter_dimension=0, tiled...  187 us
    reduce_scatter x2, waiting for transfers between devices, body(): lax.psum_scatter(key_term.reshape(groups, length, half_heads * head), 'ct...  149 us
    ppermute x7, waiting for transfers between devices, body(): later.append(lax.ppermute(later[-1], 'ctx', down))  105 us
    unnamed x163, local copies, waits for them, and re-layouts  56.6 us
    unnamed x1, blocking collectives  41.7 us
  transfers between devices with their start and end apart: 27, of which 19 were waited for; matrix products, arithmetic and copies ran while one was open for 13% of the time, Pallas kernels for 0%

profile of v1, /device:TPU:13, one launch (start us, length us, event | category | flops | bytes accessed | tf_op | source)
XLA Modules:
  0.0 1408.9 jit_solution(8551016068747936742)
XLA Ops:
  18.2 10.1 all-gather.13.cloned.1.call-done
  28.2 3.8 fusion
  33.4 13.0 collective-permute-done
  48.7 10.9 collective-permute-done.1
  59.9 24.6 %collective-permute-done.8 = bf16[2,64,2048]{2,1,0:T(8,128)(2,1)S(1)} collective-permute-done((bf16[2,64,2048]{2,1,0:T(8,128)(2,1)S(1)}, bf16[2,64,2048]{2,1,0:T(8,128)(2,1)S(1)}, u32[]{:S(2)}, u32[]{:S(2)}) %collective-permute-start.8) | collective-permute-done | bytes 524320 | tf_op jit(solution)/shard_map/ppermute | solution.py:130
  85.9 34.0 %collective-permute-done.9 = bf16[2,64,2048]{2,1,0:T(8,128)(2,1)S(1)} collective-permute-done((bf16[2,64,2048]{2,1,0:T(8,128)(2,1)S(1)}, bf16[2,64,2048]{2,1,0:T(8,128)(2,1)S(1)}, u32[]{:S(2)}, u32[]{:S(2)}) %collective-permute-start.9) | collective-permute-done | bytes 524320 | tf_op jit(solution)/shard_map/ppermute | solution.py:130
  122.2 22.9 %collective-permute-done.10 = bf16[2,64,2048]{2,1,0:T(8,128)(2,1)} collective-permute-done((bf16[2,64,2048]{2,1,0:T(8,128)(2,1)S(1)}, bf16[2,64,2048]{2,1,0:T(8,128)(2,1)}, u32[]{:S(2)}, u32[]{:S(2)}) %collective-permute-start.10) | collective-permute-done | bytes 524320 | tf_op jit(solution)/shard_map/ppermute | solution.py:130
  146.6 16.5 %collective-permute-done.11 = bf16[2,64,2048]{2,1,0:T(8,128)(2,1)} collective-permute-done((bf16[2,64,2048]{2,1,0:T(8,128)(2,1)}, bf16[2,64,2048]{2,1,0:T(8,128)(2,1)}, u32[]{:S(2)}, u32[]{:S(2)}) %collective-permute-start.11) | collective-permute-done | bytes 524320 | tf_op jit(solution)/shard_map/ppermute | solution.py:130
  163.1 3.7 collective-permute-done.5
  169.5 6.7 collective-permute-done.12
  177.4 8.1 collective-permute-done.6
  187.8 12.7 all-gather.4
  251.5 7.8 constant_dynamic-slice_fusion.2
  259.4 6.3 copy.60
  265.7 6.2 copy.63
  271.9 2.4 fusion.22
  274.7 2.7 fusion.1
  283.7 4.8 convolution_add_fusion
  288.5 7.6 fusion.100
  296.2 3.5 multiply_reduce_fusion
  306.9 2.3 reshape.252
  309.3 2.2 reduce_sum.190
  314.6 4.7 multiply_convert_fusion
  319.4 2.7 convolution_multiply_fusion.1
  322.1 5.4 copy.74
  330.3 4.6 multiply_convert_fusion.1
  336.3 2.8 convolution_multiply_fusion.2
  339.1 5.3 copy.72
  344.5 5.4 fusion.14
  349.9 5.4 copy.76
  355.4 5.3 fusion.12
  360.7 5.5 copy.78
  366.2 3.7 fusion.80
  370.3 3.1 fusion.49
  379.4 52.8 %reduce-scatter.11.cloned.1.call-done = f32[2,64,512]{2,1,0:T(8,128)} async-done(((f32[2,1024,512]{2,1,0:T(8,128)}), f32[2,64,512]{2,1,0:T(8,128)}) %reduce-scatter.11.cloned.1.call-update) | async-done | bytes 262160 | tf_op jit(solution)/shard_map/reduce_scatter | solution.py:261
  433.1 95.9 %reduce-scatter.9.cloned.1.call-done = f32[2,64,512]{2,1,0:T(8,128)} async-done(((f32[2,1024,512]{2,1,0:T(8,128)}), f32[2,64,512]{2,1,0:T(8,128)}) %reduce-scatter.9.cloned.1.call-update) | async-done | bytes 262160 | tf_op jit(solution)/shard_map/reduce_scatter | solution.py:261
  530.8 95.3 %reduce-scatter.13.cloned.1.call-done = f32[2,64,512]{2,1,0:T(8,128)} async-done(((f32[2,1024,512]{2,1,0:T(8,128)}), f32[2,64,512]{2,1,0:T(8,128)}) %reduce-scatter.13.cloned.1.call-update) | async-done | bytes 262160 | tf_op jit(solution)/shard_map/reduce_scatter | solution.py:267
  627.8 95.4 %reduce-scatter.15.cloned.1.call-done = f32[2,64,512]{2,1,0:T(8,128)} async-done(((f32[2,1024,512]{2,1,0:T(8,128)}), f32[2,64,512]{2,1,0:T(8,128)}) %reduce-scatter.15.cloned.1.call-update) | async-done | bytes 262160 | tf_op jit(solution)/shard_map/reduce_scatter | solution.py:267
  726.9 7.4 fusion.70
  734.9 9.4 fusion.66
  744.4 9.1 fusion.93
  758.8 5.7 fusion.48
  764.6 5.2 multiply_reduce_fusion.1
  769.8 41.7 %all-reduce.9 = (f32[1024]{0:T(1024)S(1)}, f32[1024]{0:T(1024)S(1)}, f32[1024]{0:T(1024)S(1)}, f32[1024]{0:T(1024)S(1)}, f32[1024]{0:T(1024)S(1)}, /*index=5*/f3...) all-reduce(f32[1024]{0:T(1024)S(1)} %get-tuple-element.17, ...), channel_id=6, replica_groups=mesh['ctx'=16,'fsdp'=2] {'ctx','fsdp'}, use_global_device_ids=true, to_apply=%region_16.17.clone | all-reduce | flops 12288 | bytes 98304
  817.7 19.2 %reduce-scatter.19.cloned.1.call-done = f32[32,1024]{1,0:T(8,128)} async-done(((f32[1024,1024]{1,0:T(8,128)}), f32[32,1024]{1,0:T(8,128)}) %reduce-scatter.19.cloned.1.call-update) | async-done | bytes 131088 | tf_op jit(solution)/shard_map/reduce_scatter | solution.py:305
  836.9 188.4 %reduce-scatter.17.cloned.1.call-done = f32[32,3072]{1,0:T(8,128)} async-done(((f32[1024,3072]{1,0:T(8,128)}), f32[32,3072]{1,0:T(8,128)}) %reduce-scatter.17.cloned.1.call-update) | async-done | bytes 393232 | tf_op jit(solution)/shard_map/reduce_scatter | solution.py:298
  1025.3 189.1 %reduce-scatter.21.cloned.1.call-done = f32[32,4096]{1,0:T(8,128)} async-done(((f32[1024,4096]{1,0:T(8,128)}), f32[32,4096]{1,0:T(8,128)}) %reduce-scatter.21.cloned.1.call-update) | async-done | bytes 524304 | tf_op jit(solution)/shard_map/reduce_scatter | solution.py:197
  1214.4 187.4 %reduce-scatter.23.cloned.1.call-done = f32[128,1024]{1,0:T(8,128)} async-done(((f32[4096,1024]{1,0:T(8,128)}), f32[128,1024]{1,0:T(8,128)}) %reduce-scatter.23.cloned.1.call-update) | async-done | bytes 524304 | tf_op jit(solution)/shard_map/reduce_scatter | solution.py:201
  (285 shorter events, 124.9 us)
Async XLA Ops:
  7.2 6.4 copy-start.5
  7.2 6.9 copy-start.49
  7.2 8.8 copy-start.50
  7.2 21.0 %all-gather.13.cloned.1.call-start = ((), (), s32[]{:S(2)}) async-start(), calls=%async_computation.8 | async-start | bytes 9437184 | tf_op jit(solution)/shard_map/all_gather | solution.py:93
  8.0 273.2 %all-gather.15.cloned.1.call-start = ((), (), s32[]{:S(2)}) async-start(), calls=%async_computation.9 | async-start | bytes 3145728 | tf_op jit(solution)/shard_map/all_gather | solution.py:96
  8.7 274.9 %all-gather.17.cloned.1.call-start = ((), (), s32[]{:S(2)}) async-start(), calls=%async_computation.10 | async-start | bytes 12582912 | tf_op jit(solution)/shard_map/all_gather | solution.py:100
  9.4 279.0 %all-gather.19.cloned.1.call-start = ((), (), s32[]{:S(2)}) async-start(), calls=%async_computation.11 | async-start | bytes 12582912 | tf_op jit(solution)/shard_map/all_gather | solution.py:102
  13.8 18.2 %copy-start.43 = (f32[128]{0:T(128)}, f32[128]{0:T(128)S(1)}, u32[]{:S(2)}) copy-start(f32[128]{0:T(128)S(1)} %div.43) | copy-start | bytes 1540
  14.1 17.9 %copy-start.45 = (f32[128]{0:T(128)}, f32[128]{0:T(128)S(1)}, u32[]{:S(2)}) copy-start(f32[128]{0:T(128)S(1)} %rsqrt.20) | copy-start | bytes 1540
  18.1 10.1 copy-start.11
  32.0 137.0 %copy-start.55 = (s32[16,2]{0,1:T(2,128)S(1)}, s32[16,2]{0,1:T(2,128)}, u32[]{:S(2)}) copy-start(s32[16,2]{0,1:T(2,128)} %param.19) | copy-start | bytes 388
  32.0 155.7 %copy-start.40 = (s32[2,1024]{1,0:T(2,128)S(1)}, s32[2,1024]{1,0:T(2,128)}, u32[]{:S(2)}) copy-start(s32[2,1024]{1,0:T(2,128)} %param.20) | copy-start | bytes 24580
  32.0 155.8 %copy-start.51 = (bf16[512]{0:T(512)(128)(2,1)S(1)}, bf16[512]{0:T(512)(128)(2,1)}, u32[]{:S(2)}) copy-start(bf16[512]{0:T(512)(128)(2,1)} %param.27) | copy-start | bytes 3076
  32.0 168.4 %copy-start.42 = (bf16[2048]{0:T(1024)(128)(2,1)S(1)}, bf16[2048]{0:T(1024)(128)(2,1)}, u32[]{:S(2)}) copy-start(bf16[2048]{0:T(1024)(128)(2,1)} %param.31) | copy-start | bytes 12292
  32.1 170.9 %copy-start.52 = (bf16[512]{0:T(512)(128)(2,1)S(1)}, bf16[512]{0:T(512)(128)(2,1)}, u32[]{:S(2)}) copy-start(bf16[512]{0:T(512)(128)(2,1)} %param.29) | copy-start | bytes 3076
  32.1 172.7 %copy-start.53 = (bf16[512]{0:T(512)(128)(2,1)S(1)}, bf16[512]{0:T(512)(128)(2,1)}, u32[]{:S(2)}) copy-start(bf16[512]{0:T(512)(128)(2,1)} %param.28) | copy-start | bytes 3076
  32.1 14.2 %collective-permute-start = (bf16[2,64,2048]{2,1,0:T(8,128)(2,1)S(1)}, bf16[2,64,2048]{2,1,0:T(8,128)(2,1)S(1)}, u32[]{:S(2)}, u32[]{:S(2)}) collective-permute-start(bf16[2,64,2048]{2,1,0:T(8,128)(2,1)S(1)} %bitcast.101), channel_id=1, source_target_pairs={{0,2},{2,4},{4,6},{6,8},{8,10},{10,12},{12,14},{14,16},{16,18},{18... | collective-permute-start | bytes 1572872 | tf_op jit(solution)/shard_map/ppermute | solution.py:128
  46.3 13.3 collective-permute-start.1
  46.6 37.8 %collective-permute-start.8 = (bf16[2,64,2048]{2,1,0:T(8,128)(2,1)S(1)}, bf16[2,64,2048]{2,1,0:T(8,128)(2,1)S(1)}, u32[]{:S(2)}, u32[]{:S(2)}) collective-permute-start(bf16[2,64,2048]{2,1,0:T(8,128)(2,1)S(1)} %bitcast.102), channel_id=1, source_target_pairs={{0,30},{2,0},{4,2},{6,4},{8,6},{10,8},{12,10},{14,12},{16,14},{18,... | collective-permute-start | bytes 1572872 | tf_op jit(solution)/shard_map/ppermute | solution.py:130
  59.6 24.8 %collective-permute-start.2 = (bf16[2,64,2048]{2,1,0:T(8,128)(2,1)S(1)}, bf16[2,64,2048]{2,1,0:T(8,128)(2,1)S(1)}, u32[]{:S(2)}, u32[]{:S(2)}) collective-permute-start(bf16[2,64,2048]{2,1,0:T(8,128)(2,1)S(1)} %collective-permute-done.1), channel_id=1, source_target_pairs={{0,2},{2,4},{4,6},{6,8},{8,10},{10,12},{12,14},{14,16},{16,18},{18... | collective-permute-start | bytes 1572872 | tf_op jit(solution)/shard_map/ppermute | solution.py:128
  84.4 35.4 %collective-permute-start.9 = (bf16[2,64,2048]{2,1,0:T(8,128)(2,1)S(1)}, bf16[2,64,2048]{2,1,0:T(8,128)(2,1)S(1)}, u32[]{:S(2)}, u32[]{:S(2)}) collective-permute-start(bf16[2,64,2048]{2,1,0:T(8,128)(2,1)S(1)} %collective-permute-done.8), channel_id=1, source_target_pairs={{0,30},{2,0},{4,2},{6,4},{8,6},{10,8},{12,10},{14,12},{16,14},{18,... | collective-permute-start | bytes 1572872 | tf_op jit(solution)/shard_map/ppermute | solution.py:130
  84.4 60.6 %copy-start.23 = (bf16[2,64,2048]{2,1,0:T(8,128)(2,1)}, bf16[2,64,2048]{2,1,0:T(8,128)(2,1)S(1)}, u32[]{:S(2)}) copy-start(bf16[2,64,2048]{2,1,0:T(8,128)(2,1)S(1)} %collective-permute-done.2) | copy-start | bytes 1572868
  84.5 36.2 %collective-permute-start.3 = (bf16[2,64,2048]{2,1,0:T(8,128)(2,1)S(1)}, bf16[2,64,2048]{2,1,0:T(8,128)(2,1)S(1)}, u32[]{:S(2)}, u32[]{:S(2)}) collective-permute-start(bf16[2,64,2048]{2,1,0:T(8,128)(2,1)S(1)} %collective-permute-done.2), channel_id=1, source_target_pairs={{0,2},{2,4},{4,6},{6,8},{8,10},{10,12},{12,14},{14,16},{16,18},{18... | collective-permute-start | bytes 1572872 | tf_op jit(solution)/shard_map/ppermute | solution.py:128
  120.7 24.3 %collective-permute-start.10 = (bf16[2,64,2048]{2,1,0:T(8,128)(2,1)S(1)}, bf16[2,64,2048]{2,1,0:T(8,128)(2,1)}, u32[]{:S(2)}, u32[]{:S(2)}) collective-permute-start(bf16[2,64,2048]{2,1,0:T(8,128)(2,1)S(1)} %collective-permute-done.9), channel_id=1, source_target_pairs={{0,30},{2,0},{4,2},{6,4},{8,6},{10,8},{12,10},{14,12},{16,14},{18,... | collective-permute-start | bytes 1572872 | tf_op jit(solution)/shard_map/ppermute | solution.py:130
  120.7 24.3 %copy-start.25 = (bf16[2,64,2048]{2,1,0:T(8,128)(2,1)}, bf16[2,64,2048]{2,1,0:T(8,128)(2,1)S(1)}, u32[]{:S(2)}) copy-start(bf16[2,64,2048]{2,1,0:T(8,128)(2,1)S(1)} %collective-permute-done.3) | copy-start | bytes 1572868
  120.7 24.3 %collective-permute-start.4 = (bf16[2,64,2048]{2,1,0:T(8,128)(2,1)S(1)}, bf16[2,64,2048]{2,1,0:T(8,128)(2,1)}, u32[]{:S(2)}, u32[]{:S(2)}) collective-permute-start(bf16[2,64,2048]{2,1,0:T(8,128)(2,1)S(1)} %collective-permute-done.3), channel_id=1, source_target_pairs={{0,2},{2,4},{4,6},{6,8},{8,10},{10,12},{12,14},{14,16},{16,18},{18... | collective-permute-start | bytes 1572872 | tf_op jit(solution)/shard_map/ppermute | solution.py:128
  145.0 18.1 %collective-permute-start.11 = (bf16[2,64,2048]{2,1,0:T(8,128)(2,1)}, bf16[2,64,2048]{2,1,0:T(8,128)(2,1)}, u32[]{:S(2)}, u32[]{:S(2)}) collective-permute-start(bf16[2,64,2048]{2,1,0:T(8,128)(2,1)} %collective-permute-done.10), channel_id=1, source_target_pairs={{0,30},{2,0},{4,2},{6,4},{8,6},{10,8},{12,10},{14,12},{16,14},{18,... | collective-permute-start | bytes 1572872 | tf_op jit(solution)/shard_map/ppermute | solution.py:130
  145.0 21.8 %collective-permute-start.5 = (bf16[2,64,2048]{2,1,0:T(8,128)(2,1)}, bf16[2,64,2048]{2,1,0:T(8,128)(2,1)}, u32[]{:S(2)}, u32[]{:S(2)}) collective-permute-start(bf16[2,64,2048]{2,1,0:T(8,128)(2,1)} %collective-permute-done.4), channel_id=1, source_target_pairs={{0,2},{2,4},{4,6},{6,8},{8,10},{10,12},{12,14},{14,16},{16,18},{18... | collective-permute-start | bytes 1572872 | tf_op jit(solution)/shard_map/ppermute | solution.py:128
  146.5 285.6 %reduce-scatter.11.cloned.1.call-start = ((), (), s32[]{:S(2)}) async-start(), calls=%async_computation.13 | async-start | bytes 4456448 | tf_op jit(solution)/shard_map/reduce_scatter | solution.py:261
  163.1 13.1 collective-permute-start.12
  166.8 18.7 %collective-permute-start.6 = (bf16[2,64,2048]{2,1,0:T(8,128)(2,1)}, bf16[2,64,2048]{2,1,0:T(8,128)(2,1)}, u32[]{:S(2)}, u32[]{:S(2)}) collective-permute-start(bf16[2,64,2048]{2,1,0:T(8,128)(2,1)} %collective-permute-done.5), channel_id=1, source_target_pairs={{0,2},{2,4},{4,6},{6,8},{8,10},{10,12},{12,14},{14,16},{16,18},{18... | collective-permute-start | bytes 1572872 | tf_op jit(solution)/shard_map/ppermute | solution.py:128
  176.2 31.1 %collective-permute-start.13 = (bf16[2,64,2048]{2,1,0:T(8,128)(2,1)}, bf16[2,64,2048]{2,1,0:T(8,128)(2,1)}, u32[]{:S(2)}, u32[]{:S(2)}) collective-permute-start(bf16[2,64,2048]{2,1,0:T(8,128)(2,1)} %collective-permute-done.12), channel_id=1, source_target_pairs={{0,30},{2,0},{4,2},{6,4},{8,6},{10,8},{12,10},{14,12},{16,14},{18,... | collective-permute-start | bytes 1572872 | tf_op jit(solution)/shard_map/ppermute | solution.py:130
  185.5 22.5 %collective-permute-start.7 = (bf16[2,64,2048]{2,1,0:T(8,128)(2,1)}, bf16[2,64,2048]{2,1,0:T(8,128)(2,1)}, u32[]{:S(2)}, u32[]{:S(2)}) collective-permute-start(bf16[2,64,2048]{2,1,0:T(8,128)(2,1)} %collective-permute-done.6), channel_id=1, source_target_pairs={{0,2},{2,4},{4,6},{6,8},{8,10},{10,12},{12,14},{14,16},{16,18},{18... | collective-permute-start | bytes 1572872 | tf_op jit(solution)/shard_map/ppermute | solution.py:128
  207.2 8.4 copy-start.26
  207.2 9.3 copy-start.24
  207.3 64.6 %copy-start.14 = (bf16[2,64,8,64]{3,2,1,0:T(8,128)(2,1)}, bf16[2,64,8,64]{3,2,1,0:T(8,128)(2,1)S(1)}, u32[]{:S(2)}) copy-start(bf16[2,64,8,64]{3,2,1,0:T(8,128)(2,1)S(1)} %get-tuple-element.43) | copy-start | bytes 393220
  207.3 67.0 %copy-start.27 = (bf16[2,64,8,64]{3,2,1,0:T(8,128)(2,1)}, bf16[2,64,8,64]{3,2,1,0:T(8,128)(2,1)S(1)}, u32[]{:S(2)}) copy-start(bf16[2,64,8,64]{3,2,1,0:T(8,128)(2,1)S(1)} %get-tuple-element.42) | copy-start | bytes 393220
  207.3 21.6 %collective-permute-start.14 = (bf16[2,64,2048]{2,1,0:T(8,128)(2,1)}, bf16[2,64,2048]{2,1,0:T(8,128)(2,1)S(1)}, u32[]{:S(2)}, u32[]{:S(2)}) collective-permute-start(bf16[2,64,2048]{2,1,0:T(8,128)(2,1)} %collective-permute-done.13), channel_id=1, source_target_pairs={{0,30},{2,0},{4,2},{6,4},{8,6},{10,8},{12,10},{14,12},{16,14},{18,... | collective-permute-start | bytes 1572872 | tf_op jit(solution)/shard_map/ppermute | solution.py:130
  211.8 8.8 copy-start.22
  283.6 12.5 copy-start.34
  288.5 7.7 copy-start
  327.5 201.6 %reduce-scatter.9.cloned.1.call-start = ((), (), s32[]{:S(2)}) async-start(), calls=%async_computation.12 | async-start | bytes 4456448 | tf_op jit(solution)/shard_map/reduce_scatter | solution.py:261
  344.4 281.7 %reduce-scatter.13.cloned.1.call-start = ((), (), s32[]{:S(2)}) async-start(), calls=%async_computation.14 | async-start | bytes 4456448 | tf_op jit(solution)/shard_map/reduce_scatter | solution.py:267
  355.4 367.9 %reduce-scatter.15.cloned.1.call-start = ((), (), s32[]{:S(2)}) async-start(), calls=%async_computation.15 | async-start | bytes 4456448 | tf_op jit(solution)/shard_map/reduce_scatter | solution.py:267
  366.2 470.7 %reduce-scatter.19.cloned.1.call-start = ((), (), s32[]{:S(2)}) async-start(), calls=%async_computation.17 | async-start | bytes 4325376 | tf_op jit(solution)/shard_map/reduce_scatter | solution.py:305
  370.0 655.3 %reduce-scatter.17.cloned.1.call-start = ((), (), s32[]{:S(2)}) async-start(), calls=%async_computation.16 | async-start | bytes 12976128 | tf_op jit(solution)/shard_map/reduce_scatter | solution.py:298
  734.3 480.0 %reduce-scatter.21.cloned.1.call-start = ((), (), s32[]{:S(2)}) async-start(), calls=%async_computation.18 | async-start | bytes 17301504 | tf_op jit(solution)/shard_map/reduce_scatter | solution.py:197
  744.4 657.4 %reduce-scatter.23.cloned.1.call-start = ((), (), s32[]{:S(2)}) async-start(), calls=%async_computation.19 | async-start | bytes 17301504 | tf_op jit(solution)/shard_map/reduce_scatter | solution.py:201
  (35 other events, 125.2 us)
Sparse Core Ops, SparseCore 0:
  9.6 18.5 all-gather.12
  29.7 11.7 all-gather.14
  43.1 21.0 all-gather.16
  146.6 20.6 all-gather.18
  327.6 104.5 reduce-scatter.10
  434.3 94.7 reduce-scatter.8
  531.4 94.7 reduce-scatter.12
  628.4 94.7 reduce-scatter.14
  726.1 110.8 reduce-scatter.18
  843.4 181.8 reduce-scatter.16
  1028.2 186.1 reduce-scatter.20
  1217.1 184.6 reduce-scatter.22
